TPU v7x, 32 devices: a whole 2x2x4 slice. The times are simulated.
32 devices in a mesh: dom: 8 (over z, y), hub: 4 (over x, core).
Axes of the slice: x: 2, y: 2, z: 4, core: 2. Of those that a mesh axis runs over, the one named last changes fastest.
Arguments:
- node_feats: bfloat16 [8, 4, 2048, 256], P('dom', 'hub'), may hold values from -6 to 6
- hub_feats: bfloat16 [1024, 256], P('hub'), may hold values from -6 to 6
- w_self: bfloat16 [256, 256], replicated, may hold values from -0.375 to 0.375
- w_neigh: bfloat16 [256, 256], replicated, may hold values from -0.375 to 0.375
- out_bias: float32 [256], replicated, may hold values from -3 to 3
- send_rows: int32 [8, 4, 8, 32], P('dom', 'hub'), may hold values from 0 to 2047, as said below
- send_counts: int32 [8, 4, 8], P('dom', 'hub'), may hold values from 0 to 32, as said below
- local_ids: int32 [8, 4, 16, 3], P('dom', 'hub'), may hold values from 0 to 15
- local_tiles: bfloat16 [8, 4, 16, 3, 128, 128], P('dom', 'hub'), may hold values from -0.5 to 0.5
- halo_ids: int32 [8, 4, 16, 2], P('dom', 'hub'), may hold values from 0 to 1
- halo_tiles: bfloat16 [8, 4, 16, 2, 128, 128], P('dom', 'hub'), may hold values from -0.5 to 0.5
- hub_ids: int32 [8, 4, 16, 2], P('dom', 'hub'), may hold values from 0 to 7
- hub_tiles: bfloat16 [8, 4, 16, 2, 128, 128], P('dom', 'hub'), may hold values from -0.5 to 0.5
- degree: int32 [8, 4, 2048], P('dom', 'hub'), may hold values from 1 to 8
- out_grad: bfloat16 [8, 4, 2048, 256], P('dom', 'hub'), may hold values from -6 to 6
Outputs:
- layer_out: bfloat16 [8, 4, 2048, 256], P('dom', 'hub')
- feats_grad: bfloat16 [8, 4, 2048, 256], P('dom', 'hub')
- grad_self: float32 [256, 256], replicated
- grad_neigh: float32 [256, 256], replicated
- grad_bias: float32 [256], replicated
- hub_grads: float32 [1024, 256], P('hub')
Inputs may be any that keep to these rules, and one draw needn't show every extreme that they name: `send_rows`: entry [p, h, a, s] is a row of partition (p, h) that it sends to partition (a, h) in slot s; only the first send_counts[p, h, a] slots of a list are used. `send_counts`: a partition sends nothing to itself; each partition sends 32 rows to at least one peer and receives 32 rows from at least one peer.
All inputs are finite; a program needn't handle non-finite values.
Results may differ from a plain program's by a relative error of at most 0.0056.
Values may be sent and summed in bfloat16 or wider, within the bound.
A program may use at most 128 MiB of HBM per device.

v0:
```python
import math
import jax
import jax.numpy as jnp
from jax import lax
from jax.sharding import PartitionSpec as P


def block_apply(tile_set, sources):
    return jnp.einsum("bkij,bkjf->bif", tile_set, sources, preferred_element_type=jnp.float32)


def block_spread(tile_set, grad_blocks):
    return jnp.einsum("bkij,bif->bkjf", tile_set, grad_blocks, preferred_element_type=jnp.float32)


def silu_slope(preact):
    sigmoid = jax.nn.sigmoid(preact)
    return sigmoid * (1.0 + preact * (1.0 - sigmoid))


def collect_blocks(pieces, index_table, block_total):
    flat_parts = pieces.reshape(
        pieces.shape[0] * pieces.shape[1], pieces.shape[2] * pieces.shape[3]
    )
    wanted = lax.broadcasted_iota(jnp.int32, (block_total, 1), 0)
    onehot = (index_table.reshape(1, -1) == wanted).astype(jnp.float32)
    return jnp.dot(
        onehot, flat_parts, precision=lax.Precision.HIGHEST, preferred_element_type=jnp.float32
    )


def body(
    node_feats,
    hub_feats,
    w_self,
    w_neigh,
    out_bias,
    send_rows,
    send_counts,
    local_ids,
    local_tiles,
    halo_ids,
    halo_tiles,
    hub_ids,
    hub_tiles,
    degree,
    out_grad,
):
    row_count = node_feats.shape[2]
    feat_width = node_feats.shape[3]
    tile_size = local_tiles.shape[-1]
    block_count = row_count // tile_size
    peer_count = lax.axis_size("dom")
    loop_count = lax.axis_size("hub")
    features = node_feats.reshape(row_count, feat_width)
    send_index = send_rows.reshape(peer_count, -1)
    slot_count = send_index.shape[1]
    send_live = lax.broadcasted_iota(jnp.int32, (peer_count, slot_count), 1) < send_counts.reshape(
        peer_count, 1
    )
    outgoing = jnp.where(send_live[:, :, None], features[send_index], jnp.zeros((), features.dtype))
    halo_rows = lax.all_to_all(outgoing, "dom", split_axis=0, concat_axis=0, tiled=True)
    hub_all = lax.all_gather(hub_feats, "hub", axis=0, tiled=True)
    local_index = local_ids[0, 0]
    local_tile = local_tiles[0, 0]
    halo_index = halo_ids[0, 0]
    halo_tile = halo_tiles[0, 0]
    hub_index = hub_ids[0, 0]
    hub_tile = hub_tiles[0, 0]
    summed = block_apply(
        local_tile, features.reshape(block_count, tile_size, feat_width)[local_index]
    )
    summed = summed + block_apply(
        halo_tile, halo_rows.reshape(-1, tile_size, feat_width)[halo_index]
    )
    summed = summed + block_apply(hub_tile, hub_all.reshape(-1, tile_size, feat_width)[hub_index])
    row_scale = 1.0 / degree.reshape(row_count).astype(jnp.float32)
    aggregate = (summed.reshape(row_count, feat_width) * row_scale[:, None]).astype(jnp.bfloat16)
    preact = (
        jnp.dot(features, w_self, preferred_element_type=jnp.float32)
        + jnp.dot(aggregate, w_neigh, preferred_element_type=jnp.float32)
        + out_bias
    )
    layer_rows = jax.nn.silu(preact).astype(jnp.bfloat16)
    grad_pre = (
        out_grad.reshape(row_count, feat_width).astype(jnp.float32) * silu_slope(preact)
    ).astype(jnp.bfloat16)
    contract_rows = (((0,), (0,)), ((), ()))
    contract_cols = (((1,), (1,)), ((), ()))
    part_self = lax.dot_general(
        features, grad_pre, contract_rows, preferred_element_type=jnp.float32
    )
    part_neigh = lax.dot_general(
        aggregate, grad_pre, contract_rows, preferred_element_type=jnp.float32
    )
    part_bias = jnp.sum(grad_pre.astype(jnp.float32), axis=0)
    total_self, total_neigh, total_bias = lax.psum(
        (part_self, part_neigh, part_bias), ("dom", "hub")
    )
    factor = 1.0 / math.sqrt(row_count * peer_count * loop_count)
    direct = lax.dot_general(grad_pre, w_self, contract_cols, preferred_element_type=jnp.float32)
    grad_scaled = lax.dot_general(
        grad_pre, w_neigh, contract_cols, preferred_element_type=jnp.float32
    )
    grad_scaled = (
        (grad_scaled * row_scale[:, None])
        .astype(jnp.bfloat16)
        .reshape(block_count, tile_size, feat_width)
    )
    halo_back = collect_blocks(
        block_spread(halo_tile, grad_scaled), halo_index, peer_count * slot_count // tile_size
    )
    returned = lax.all_to_all(
        halo_back.reshape(peer_count, slot_count, feat_width),
        "dom",
        split_axis=0,
        concat_axis=0,
        tiled=True,
    )
    local_back = collect_blocks(block_spread(local_tile, grad_scaled), local_index, block_count)
    own_grad = direct + local_back.reshape(row_count, feat_width)
    returned = jnp.where(send_live[:, :, None], returned, jnp.zeros((), returned.dtype))
    own_grad = own_grad.at[send_index.reshape(-1)].add(returned.reshape(-1, feat_width))
    hub_pieces = block_spread(hub_tile, grad_scaled)
    hub_dev_rows = hub_feats.shape[0]
    own_blocks = hub_dev_rows // tile_size
    full_sum = collect_blocks(hub_pieces, hub_index, own_blocks * loop_count)
    full_sum = lax.psum(full_sum, ("dom", "hub"))
    my_share = lax.dynamic_slice_in_dim(full_sum, lax.axis_index("hub") * own_blocks, own_blocks, 0)
    hub_grads = my_share.reshape(hub_dev_rows, feat_width)
    return (
        layer_rows.reshape(node_feats.shape),
        own_grad.astype(jnp.bfloat16).reshape(node_feats.shape),
        total_self * factor,
        total_neigh * factor,
        total_bias * factor,
        hub_grads,
    )


def solution(mesh):
    placed = (
        P("dom", "hub", None, None),
        P("hub", None),
        P(),
        P(),
        P(),
        P("dom", "hub", None, None),
        P("dom", "hub", None),
        P("dom", "hub", None, None),
        P("dom", "hub", None, None, None, None),
        P("dom", "hub", None, None),
        P("dom", "hub", None, None, None, None),
        P("dom", "hub", None, None),
        P("dom", "hub", None, None, None, None),
        P("dom", "hub", None),
        P("dom", "hub", None, None),
    )
    return jax.shard_map(
        body,
        mesh=mesh,
        in_specs=placed,
        out_specs=(
            P("dom", "hub", None, None),
            P("dom", "hub", None, None),
            P(),
            P(),
            P(),
            P("hub", None),
        ),
        check_vma=False,
    )
```

profile of v0, /device:TPU:0, one launch (start us, length us, event | category | flops | bytes accessed | tf_op | source)
XLA Modules:
  0.0 287.2 jit_solution(3315615849919298533)
XLA Ops:
  8.9 2.3 gather_fusion.1
  12.0 7.3 %all-to-all-start = ((bf16[8,32,256]{2,1,0:T(8,128)(2,1)}), bf16[8,32,256]{2,1,0:T(8,128)(2,1)S(1)}, u32[]{:S(2)}, u32[]{:S(2)}) async-start(bf16[8,32,256]{2,1,0:T(8,128)(2,1)} %broadcast_select_fusion.1), calls=%async_computation | async-start | bytes 262144 | tf_op jit(solution)/shard_map/all_to_all | solution.py:62
  22.6 7.4 %all_gather.3 = bf16[1024,256]{1,0:T(8,128)(2,1)S(1)} all-gather(bf16[256,256]{1,0:T(8,128)(2,1)} %param.16), channel_id=1, replica_groups=mesh['dom'=8,'hub'=4] {'hub'}, dimensions={0}, use_global_device_ids=true | all-gather | bytes 655360 | tf_op jit(solution)/shard_map/all_gather | solution.py:63
  31.7 2.5 gather_fusion
  34.3 4.0 %fusion.5 = f32[16,256,128,1]{1,2,3,0:T(8,128)} fusion(bf16[16,3,128,256]{3,2,1,0:T(8,128)(2,1)} %bitcast.139, bf16[1,1,16,3,128,128]{5,4,3,2,1,0:T(8,128)(2,1)S(1)} %copy-done), kind=kOutput, calls=%fused_computation.23 | convolution fusion | flops 402653184 | bytes 6815744 | tf_op jit(solution)/shard_map/bkij,bkjf->bif/dot_general | solution.py:9
  38.9 2.0 gather_fusion.3
  40.9 2.0 gather_fusion.2
  43.0 2.6 fusion.10
  48.7 2.2 convert_reduce_fusion
  53.8 2.7 convolution_bitcast_fusion.1
  56.6 2.8 convolution_bitcast_fusion.2
  59.4 3.7 %convolution_bitcast_fusion = f32[16,3,128,256]{2,3,1,0:T(8,128)} fusion(bf16[16,128,256,1]{2,1,3,0:T(8,128)(2,1)S(1)} %bitcast.137, bf16[1,1,16,3,128,128]{5,4,3,2,1,0:T(8,128)(2,1)S(1)} %copy-done), kind=kOutput, calls=%fused_computation.9 | convolution fusion | flops 402653184 | bytes 8912896 | tf_op jit(solution)/shard_map/bkij,bif->bkjf/dot_general | solution.py:13
  63.1 40.2 %psum.30 = f32[256]{0:T(256)S(1)} all-reduce(f32[256]{0:T(256)S(1)} %get-tuple-element.21), channel_id=1, replica_groups=mesh['dom'=8,'hub'=4] {'dom','hub'}, use_global_device_ids=true, to_apply=%region_4.5 | all-reduce | flops 256 | bytes 2048 | tf_op jit(solution)/shard_map/psum | solution.py:97
  103.3 5.5 %copy.63 = f32[4,8,128,256]{3,1,2,0:T(8,128)} copy(f32[4,8,128,256]{2,3,1,0:T(8,128)} %bitcast.133) | data formatting | bytes 8388608
  108.8 5.5 %copy.62 = f32[4,8,128,256]{3,1,2,0:T(8,128)} copy(f32[4,8,128,256]{2,3,1,0:T(8,128)} %bitcast.132) | data formatting | bytes 8388608
  114.3 3.6 %fusion.17 = f32[2,32768]{1,0:T(2,128)S(1)} fusion(f32[32,32768]{1,0:T(8,128)} %bitcast.134, s32[32]{0:T(128)S(1)} %eq.49), kind=kOutput, calls=%fused_computation.54 | convolution fusion | flops 25165888 | bytes 4456576 | tf_op jit(solution)/shard_map/dot_general | solution.py:27
  118.8 5.3 %all-to-all-start.1 = ((f32[8,32,256]{2,1,0:T(8,128)}), f32[8,32,256]{2,1,0:T(8,128)S(1)}, u32[]{:S(2)}, u32[]{:S(2)}) async-start(f32[8,32,256]{2,1,0:T(8,128)} %reshape.247), calls=%async_computation.1 | async-start | bytes 524288 | tf_op jit(solution)/shard_map/all_to_all | solution.py:113
  124.1 6.6 %copy.61 = f32[6,8,128,256]{3,1,2,0:T(8,128)} copy(f32[6,8,128,256]{2,3,1,0:T(8,128)} %bitcast.129) | data formatting | bytes 12582912
  130.7 4.2 %fusion.13 = f32[16,32768]{1,0:T(8,128)S(1)} fusion(f32[48,32768]{1,0:T(8,128)} %bitcast.130, s32[48]{0:T(128)S(1)} %eq.45), kind=kOutput, calls=%fused_computation.41 | convolution fusion | flops 301990656 | bytes 8388800 | tf_op jit(solution)/shard_map/dot_general | solution.py:27
  136.4 4.6 %fusion.15 = f32[8,32768]{1,0:T(8,128)} fusion(f32[32,32768]{1,0:T(8,128)} %bitcast.131, s32[32]{0:T(128)S(1)} %eq.53), kind=kOutput, calls=%fused_computation.50 | convolution fusion | flops 100663552 | bytes 5243008 | tf_op jit(solution)/shard_map/dot_general | solution.py:27
  142.3 3.4 %convolution_add_fusion = f32[2048,256]{1,0:T(8,128)} fusion(f32[2048,256]{1,0:T(8,128)} %reshape.245, bf16[2048,256]{1,0:T(8,128)(2,1)S(1)} %copy-done.4, bf16[256,256]{1,0:T(8,128)(2,1)S(1)} %copy-done.10), kind=kOutput, calls=%fused_computation.6 | convolution fusion | flops 268959744 | bytes 5373952 | tf_op jit(solution)/shard_map/dot_general | solution.py:101
  146.3 4.7 %scatter_fusion = f32[2048,256]{1,0:T(8,128)} fusion(f32[2048,256]{1,0:T(8,128)} %convolution_add_fusion, s32[256]{0:T(256)S(1)} %bitcast.146, f32[256,256]{1,0:T(8,128)S(1)} %bitcast.142), kind=kCustom, calls=%fused_computation.4 | custom fusion | flops 65536 | bytes 787456 | tf_op jit(solution)/shard_map/scatter-add | solution.py:123
  151.0 2.8 convert_bitcast_fusion
  153.8 121.6 %all-reduce.3.cloned.1.call-done = (f32[256,256]{0,1:T(8,128)}, f32[256,256]{0,1:T(8,128)}, f32[8,32768]{1,0:T(8,128)}) async-done(((f32[256,256]{0,1:T(8,128)}, f32[256,256]{0,1:T(8,128)}, f32[8,32768]{1,0:T(8,128)}), (f32[256,256]{0,1:T(8,128)}, f32[256,256]{0,1:T(8,128)}, f32[8,32768]{1,0:T(8,128)})) %all-reduce.3.cloned.1.call-update) | async-done | bytes 1572880 | tf_op jit(solution)/shard_map/psum | solution.py:97
  (81 shorter events, 23.5 us)
Async XLA Ops:
  7.2 27.1 %copy-start = (bf16[1,1,16,3,128,128]{5,4,3,2,1,0:T(8,128)(2,1)S(1)}, bf16[1,1,16,3,128,128]{5,4,3,2,1,0:T(8,128)(2,1)}, u32[]{:S(2)}) copy-start(bf16[1,1,16,3,128,128]{5,4,3,2,1,0:T(8,128)(2,1)} %param.23) | copy-start | bytes 4718596
  7.2 22.8 %copy-start.2 = (bf16[1,1,2048,256]{3,2,1,0:T(8,128)(2,1)S(1)}, bf16[1,1,2048,256]{3,2,1,0:T(8,128)(2,1)}, u32[]{:S(2)}) copy-start(bf16[1,1,2048,256]{3,2,1,0:T(8,128)(2,1)} %param.15) | copy-start | bytes 3145732
  7.2 22.7 %copy-start.10 = (bf16[256,256]{1,0:T(8,128)(2,1)S(1)}, bf16[256,256]{1,0:T(8,128)(2,1)}, u32[]{:S(2)}) copy-start(bf16[256,256]{1,0:T(8,128)(2,1)} %param.17) | copy-start | bytes 393220
  12.0 29.0 %all-to-all-start = ((bf16[8,32,256]{2,1,0:T(8,128)(2,1)}), bf16[8,32,256]{2,1,0:T(8,128)(2,1)S(1)}, u32[]{:S(2)}, u32[]{:S(2)}) async-start(bf16[8,32,256]{2,1,0:T(8,128)(2,1)} %broadcast_select_fusion.1), calls=%async_computation | async-start | bytes 262144 | tf_op jit(solution)/shard_map/all_to_all | solution.py:62
  34.3 4.0 %copy-start.12 = (s32[1,1,8,32]{3,2,1,0:T(8,128)S(1)}, s32[1,1,8,32]{3,2,1,0:T(8,128)}, u32[]{:S(2)}) copy-start(s32[1,1,8,32]{3,2,1,0:T(8,128)} %param.20) | copy-start | bytes 3076
  34.3 4.1 %copy-start.13 = (s32[1,1,16,3]{2,1,3,0:T(1,128)S(1)}, s32[1,1,16,3]{2,1,3,0:T(1,128)}, u32[]{:S(2)}) copy-start(s32[1,1,16,3]{2,1,3,0:T(1,128)} %param.22) | copy-start | bytes 580
  34.3 4.2 %copy-start.14 = (s32[1,1,16,2]{2,3,1,0:T(2,128)S(1)}, s32[1,1,16,2]{2,3,1,0:T(2,128)}, u32[]{:S(2)}) copy-start(s32[1,1,16,2]{2,3,1,0:T(2,128)} %param.24) | copy-start | bytes 388
  34.3 4.2 %copy-start.15 = (s32[1,1,16,2]{2,3,1,0:T(2,128)S(1)}, s32[1,1,16,2]{2,3,1,0:T(2,128)}, u32[]{:S(2)}) copy-start(s32[1,1,16,2]{2,3,1,0:T(2,128)} %param.26) | copy-start | bytes 388
  42.9 2.6 copy-start.5
  42.9 3.2 %copy-start.6 = (bf16[32,128,256]{2,1,0:T(8,128)(2,1)S(1)}, bf16[32,128,256]{2,1,0:T(8,128)(2,1)}, u32[]{:S(2)}) copy-start(bf16[32,128,256]{2,1,0:T(8,128)(2,1)} %gather_fusion.3) | copy-start | bytes 6291460
  43.0 3.4 %copy-start.7 = (bf16[1,1,16,2,128,128]{5,4,3,2,1,0:T(8,128)(2,1)S(1)}, bf16[1,1,16,2,128,128]{5,4,3,2,1,0:T(8,128)(2,1)}, u32[]{:S(2)}) copy-start(bf16[1,1,16,2,128,128]{5,4,3,2,1,0:T(8,128)(2,1)} %param.27) | copy-start | bytes 3145732
  46.4 1.2 copy-start.16
  47.0 1.7 copy-start.9
  47.0 1.7 copy-start.11
  47.0 1.7 copy-start.17
  50.9 2.4 copy-start.3
  53.8 2.7 copy-start.8
  118.8 27.4 %all-to-all-start.1 = ((f32[8,32,256]{2,1,0:T(8,128)}), f32[8,32,256]{2,1,0:T(8,128)S(1)}, u32[]{:S(2)}, u32[]{:S(2)}) async-start(f32[8,32,256]{2,1,0:T(8,128)} %reshape.247), calls=%async_computation.1 | async-start | bytes 524288 | tf_op jit(solution)/shard_map/all_to_all | solution.py:113
  124.1 151.3 %all-reduce.3.cloned.1.call-start = ((), (), s32[]{:S(2)}) async-start(), calls=%async_computation.2 | async-start | bytes 3145728 | tf_op jit(solution)/shard_map/psum | solution.py:97
  141.0 1.2 copy-start.4
  151.0 129.4 %copy-start.1 = (bf16[1,1,16,3,128,128]{5,4,3,2,1,0:T(8,128)(2,1)S(1)}, bf16[1,1,16,3,128,128]{5,4,3,2,1,0:T(8,128)(2,1)}, u32[]{:S(2)}) copy-start(bf16[1,1,16,3,128,128]{5,4,3,2,1,0:T(8,128)(2,1)} %param.23) | copy-start | bytes 4718596
Sparse Core Ops, SparseCore 0:
  141.2 134.1 all-reduce.2
where the time goes:
time: 288 us; the launch traced here: 287 us
  waiting for transfers between devices  122 us (42%)
  blocking collectives  47.6 us (17%)
  matrix products  39 us (14%)
  local copies, waits for them, and re-layouts  37.5 us (13%)
  other arithmetic  14.7 us (5%)
  between operations  14.2 us (5%)
  starting transfers between devices  12.6 us (4%)
    psum x1, waiting for transfers between devices, body(): lax.psum((part_self, part_neigh, part_bias), ('dom', 'hub'))  122 us
    psum x1, blocking collectives, body(): lax.psum((part_self, part_neigh, part_bias), ('dom', 'hub'))  40.2 us
    unnamed x44, local copies, waits for them, and re-layouts  22.9 us
    dot_general x3, matrix products, collect_blocks(): jnp.dot(onehot, flat_parts, precision=lax.Precision.HIGHEST, preferred_el...  12.4 us
    dot_general x3, matrix products, block_spread(): jnp.einsum('bkij,bif->bkjf', tile_set, grad_blocks, preferred_element_typ...  9.24 us
    all_gather x1, blocking collectives, body(): hub_all = lax.all_gather(hub_feats, 'hub', axis=0, tiled=True)  7.38 us
    all_to_all x1, starting transfers between devices, body(): lax.all_to_all(outgoing, 'dom', split_axis=0, concat_axis=0, tiled=True)  7.28 us
    dot_general x3, matrix products, block_apply(): jnp.einsum('bkij,bkjf->bif', tile_set, sources, preferred_element_type=jn...  7.16 us
  transfers between devices with their start and end apart: 3, of which 1 were waited for; matrix products, arithmetic and copies ran while one was open for 15% of the time, Pallas kernels for 0%

commit v1 on v0

--- a/solution.py
+++ b/solution.py
@@ -3,6 +3,19 @@
 import jax.numpy as jnp
 from jax import lax
 from jax.sharding import PartitionSpec as P
+
+
+def ring_gather(x, axis, dim):
+    ways = lax.axis_size(axis)
+    up = [(d, (d + 1) % ways) for d in range(ways)]
+    down = [(d, (d - 1) % ways) for d in range(ways)]
+    earlier, later = ([x], [x])
+    for _ in range(ways // 2):
+        earlier.append(lax.ppermute(earlier[-1], axis, up))
+    for _ in range((ways - 1) // 2):
+        later.append(lax.ppermute(later[-1], axis, down))
+    line = jnp.concatenate([*earlier[::-1], *later[1:]], axis=dim)
+    return jnp.roll(line, (lax.axis_index(axis) - ways // 2) * x.shape[dim], axis=dim)
 
 
 def block_apply(tile_set, sources):
@@ -60,7 +73,7 @@
     )
     outgoing = jnp.where(send_live[:, :, None], features[send_index], jnp.zeros((), features.dtype))
     halo_rows = lax.all_to_all(outgoing, "dom", split_axis=0, concat_axis=0, tiled=True)
-    hub_all = lax.all_gather(hub_feats, "hub", axis=0, tiled=True)
+    hub_all = ring_gather(hub_feats, "hub", 0)
     local_index = local_ids[0, 0]
     local_tile = local_tiles[0, 0]
     halo_index = halo_ids[0, 0]

time: 288 us -> 287 us (level)
  blocking collectives: 47.6 us -> 41 us
  matrix products: 39 us -> 44.4 us
    all_gather x1 -> x0, blocking collectives: 7.38 us -> none  [body(): hub_all = lax.all_gather(hub_feats, 'hub', axis=0, tiled=True)]
    dot_general x3, matrix products: 7.16 us -> 11.6 us  [block_apply(): jnp.einsum('bkij,bkjf->bif', tile_set, sources, preferred_element_type=jn...]
    unnamed x44 -> x49, local copies, waits for them, and re-layouts: 22.9 us -> 22 us
  transfers between devices with their start and end apart: 3 -> 6, of which waited for: 1 -> 1; matrix products, arithmetic and copies ran while one was open for 15% -> 18% of each run, Pallas kernels for 0% -> 0%
where the time goes in v1:
time: 287 us; the launch traced here: 286 us
  waiting for transfers between devices  121 us (42%)
  matrix products  44.4 us (15%)
  blocking collectives  41 us (14%)
  local copies, waits for them, and re-layouts  37.3 us (13%)
  starting transfers between devices  14.4 us (5%)
  between operations  14.4 us (5%)
  other arithmetic  14 us (5%)
    psum x1, waiting for transfers between devices, body(): lax.psum((part_self, part_neigh, part_bias), ('dom', 'hub'))  121 us
    psum x1, blocking collectives, body(): lax.psum((part_self, part_neigh, part_bias), ('dom', 'hub'))  41 us
    unnamed x49, local copies, waits for them, and re-layouts  22 us
    dot_general x3, matrix products, collect_blocks(): jnp.dot(onehot, flat_parts, precision=lax.Precision.HIGHEST, preferred_el...  12.4 us
    dot_general x3, matrix products, block_apply(): jnp.einsum('bkij,bkjf->bif', tile_set, sources, preferred_element_type=jn...  11.6 us
    dot_general x3, matrix products, block_spread(): jnp.einsum('bkij,bif->bkjf', tile_set, grad_blocks, preferred_element_typ...  9.26 us
    all_to_all x1, starting transfers between devices, body(): lax.all_to_all(outgoing, 'dom', split_axis=0, concat_axis=0, tiled=True)  6.58 us
  transfers between devices with their start and end apart: 6, of which 1 were waited for; matrix products, arithmetic and copies ran while one was open for 18% of the time, Pallas kernels for 0%

profile of v1, /device:TPU:0, one launch (start us, length us, event | category | flops | bytes accessed | tf_op | source)
XLA Modules:
  0.0 286.4 jit_solution(8674665724046263068)
XLA Ops:
  12.1 2.3 gather_fusion.1
  15.1 6.6 %all-to-all-start = ((bf16[8,32,256]{2,1,0:T(8,128)(2,1)}), bf16[8,32,256]{2,1,0:T(8,128)(2,1)S(1)}, u32[]{:S(2)}, u32[]{:S(2)}) async-start(bf16[8,32,256]{2,1,0:T(8,128)(2,1)} %broadcast_select_fusion.1), calls=%async_computation | async-start | bytes 262144 | tf_op jit(solution)/shard_map/all_to_all | solution.py:75
  24.1 2.7 fusion.22
  26.8 2.5 gather_fusion
  29.3 4.0 %fusion.5 = f32[16,256,128,1]{1,2,3,0:T(8,128)} fusion(bf16[16,3,128,256]{3,2,1,0:T(8,128)(2,1)} %bitcast.139, bf16[1,1,16,3,128,128]{5,4,3,2,1,0:T(8,128)(2,1)S(1)} %copy-done), kind=kOutput, calls=%fused_computation.23 | convolution fusion | flops 402653184 | bytes 6815744 | tf_op jit(solution)/shard_map/bkij,bkjf->bif/dot_general | solution.py:22
  34.1 2.0 gather_fusion.2
  36.2 3.8 %fusion.10 = f32[16,256,128,1]{1,2,3,0:T(8,128)} fusion(bf16[16,2,128,256]{3,2,1,0:T(8,128)(2,1)} %bitcast.140, bf16[1,1,16,2,128,128]{5,4,3,2,1,0:T(8,128)(2,1)} %param.25), kind=kOutput, calls=%fused_computation.29 | convolution fusion | flops 268435456 | bytes 5242880 | tf_op jit(solution)/shard_map/bkij,bkjf->bif/dot_general | solution.py:22
  42.2 3.8 %bitcast_add_fusion = f32[16,256,128]{1,2,0:T(8,128)S(1)} fusion(f32[16,256,128,1]{1,2,3,0:T(8,128)} %fusion.10, f32[16,256,128,1]{1,2,3,0:T(8,128)} %fusion.5, bf16[16,2,128,256]{3,2,1,0:T(8,128)(2,1)} %bitcast.141, bf16[1,1,16,2,128,128]{5,4,3,2,1,0:T(8,128)(2,1)} %param.27), kind=kOutput, calls=%fused_computation.17 | convolution fusion | flops 269484032 | bytes 9437184 | tf_op jit(solution)/shard_map/bkij,bkjf->bif/dot_general | solution.py:22
  47.7 2.2 convert_reduce_fusion
  52.9 2.7 convolution_bitcast_fusion.1
  55.6 2.8 convolution_bitcast_fusion.2
  58.4 3.7 %convolution_bitcast_fusion = f32[16,3,128,256]{2,3,1,0:T(8,128)} fusion(bf16[16,128,256,1]{2,1,3,0:T(8,128)(2,1)S(1)} %bitcast.137, bf16[1,1,16,3,128,128]{5,4,3,2,1,0:T(8,128)(2,1)S(1)} %copy-done), kind=kOutput, calls=%fused_computation.9 | convolution fusion | flops 402653184 | bytes 8912896 | tf_op jit(solution)/shard_map/bkij,bif->bkjf/dot_general | solution.py:26
  62.1 41.0 %psum.30 = f32[256]{0:T(256)S(1)} all-reduce(f32[256]{0:T(256)S(1)} %get-tuple-element.21), channel_id=1, replica_groups=mesh['dom'=8,'hub'=4] {'dom','hub'}, use_global_device_ids=true, to_apply=%region_4.5 | all-reduce | flops 256 | bytes 2048 | tf_op jit(solution)/shard_map/psum | solution.py:110
  103.1 5.5 %copy.63 = f32[4,8,128,256]{3,1,2,0:T(8,128)} copy(f32[4,8,128,256]{2,3,1,0:T(8,128)} %bitcast.133) | data formatting | bytes 8388608
  108.6 5.4 %copy.62 = f32[4,8,128,256]{3,1,2,0:T(8,128)} copy(f32[4,8,128,256]{2,3,1,0:T(8,128)} %bitcast.132) | data formatting | bytes 8388608
  114.0 3.6 %fusion.17 = f32[2,32768]{1,0:T(2,128)S(1)} fusion(f32[32,32768]{1,0:T(8,128)} %bitcast.134, s32[32]{0:T(128)S(1)} %eq.52), kind=kOutput, calls=%fused_computation.62 | convolution fusion | flops 25165888 | bytes 4456576 | tf_op jit(solution)/shard_map/dot_general | solution.py:40
  118.6 5.3 %all-to-all-start.1 = ((f32[8,32,256]{2,1,0:T(8,128)}), f32[8,32,256]{2,1,0:T(8,128)S(1)}, u32[]{:S(2)}, u32[]{:S(2)}) async-start(f32[8,32,256]{2,1,0:T(8,128)} %reshape.247), calls=%async_computation.1 | async-start | bytes 524288 | tf_op jit(solution)/shard_map/all_to_all | solution.py:126
  123.9 6.6 %copy.61 = f32[6,8,128,256]{3,1,2,0:T(8,128)} copy(f32[6,8,128,256]{2,3,1,0:T(8,128)} %bitcast.129) | data formatting | bytes 12582912
  130.5 4.2 %fusion.13 = f32[16,32768]{1,0:T(8,128)S(1)} fusion(f32[48,32768]{1,0:T(8,128)} %bitcast.130, s32[48]{0:T(128)S(1)} %eq.48), kind=kOutput, calls=%fused_computation.49 | convolution fusion | flops 301990656 | bytes 8388800 | tf_op jit(solution)/shard_map/dot_general | solution.py:40
  136.2 4.6 %fusion.15 = f32[8,32768]{1,0:T(8,128)} fusion(f32[32,32768]{1,0:T(8,128)} %bitcast.131, s32[32]{0:T(128)S(1)} %eq.56), kind=kOutput, calls=%fused_computation.58 | convolution fusion | flops 100663552 | bytes 5243008 | tf_op jit(solution)/shard_map/dot_general | solution.py:40
  142.0 3.4 %convolution_add_fusion = f32[2048,256]{1,0:T(8,128)} fusion(f32[2048,256]{1,0:T(8,128)} %reshape.245, bf16[2048,256]{1,0:T(8,128)(2,1)S(1)} %copy-done.4, bf16[256,256]{1,0:T(8,128)(2,1)S(1)} %copy-done.9), kind=kOutput, calls=%fused_computation.6 | convolution fusion | flops 268959744 | bytes 5373952 | tf_op jit(solution)/shard_map/dot_general | solution.py:114
  146.1 4.8 %scatter_fusion = f32[2048,256]{1,0:T(8,128)} fusion(f32[2048,256]{1,0:T(8,128)} %convolution_add_fusion, s32[256]{0:T(256)S(1)} %bitcast.146, f32[256,256]{1,0:T(8,128)S(1)} %bitcast.142), kind=kCustom, calls=%fused_computation.4 | custom fusion | flops 65536 | bytes 787456 | tf_op jit(solution)/shard_map/scatter-add | solution.py:136
  150.9 2.8 convert_bitcast_fusion
  153.7 120.8 %all-reduce.3.cloned.1.call-done = (f32[256,256]{0,1:T(8,128)}, f32[256,256]{0,1:T(8,128)}, f32[8,32768]{1,0:T(8,128)}) async-done(((f32[256,256]{0,1:T(8,128)}, f32[256,256]{0,1:T(8,128)}, f32[8,32768]{1,0:T(8,128)}), (f32[256,256]{0,1:T(8,128)}, f32[256,256]{0,1:T(8,128)}, f32[8,32768]{1,0:T(8,128)})) %all-reduce.3.cloned.1.call-update) | async-done | bytes 1572880 | tf_op jit(solution)/shard_map/psum | solution.py:110
  (93 shorter events, 24.7 us)
Async XLA Ops:
  7.2 22.2 %copy-start = (bf16[1,1,16,3,128,128]{5,4,3,2,1,0:T(8,128)(2,1)S(1)}, bf16[1,1,16,3,128,128]{5,4,3,2,1,0:T(8,128)(2,1)}, u32[]{:S(2)}) copy-start(bf16[1,1,16,3,128,128]{5,4,3,2,1,0:T(8,128)(2,1)} %param.23) | copy-start | bytes 4718596
  7.2 16.9 %copy-start.2 = (bf16[1,1,2048,256]{3,2,1,0:T(8,128)(2,1)S(1)}, bf16[1,1,2048,256]{3,2,1,0:T(8,128)(2,1)}, u32[]{:S(2)}) copy-start(bf16[1,1,2048,256]{3,2,1,0:T(8,128)(2,1)} %param.15) | copy-start | bytes 3145732
  7.2 26.8 %collective-permute-start = (bf16[256,256]{1,0:T(8,128)(2,1)}, bf16[256,256]{1,0:T(8,128)(2,1)S(1)}, u32[]{:S(2)}, u32[]{:S(2)}) collective-permute-start(bf16[256,256]{1,0:T(8,128)(2,1)} %param.16), channel_id=1, source_target_pairs={{0,1},{1,2},{2,3},{3,0},{4,5},{5,6},{6,7},{7,4},{8,9},{9,10},{10,1... | collective-permute-start | bytes 393224 | tf_op jit(solution)/shard_map/ppermute | solution.py:14
  7.7 32.3 %collective-permute-start.2 = (bf16[256,256]{1,0:T(8,128)(2,1)}, bf16[256,256]{1,0:T(8,128)(2,1)S(1)}, u32[]{:S(2)}, u32[]{:S(2)}) collective-permute-start(bf16[256,256]{1,0:T(8,128)(2,1)} %param.16), channel_id=1, source_target_pairs={{0,3},{1,0},{2,1},{3,2},{4,7},{5,4},{6,5},{7,6},{8,11},{9,8},{10,9... | collective-permute-start | bytes 393224 | tf_op jit(solution)/shard_map/ppermute | solution.py:16
  15.1 19.0 %all-to-all-start = ((bf16[8,32,256]{2,1,0:T(8,128)(2,1)}), bf16[8,32,256]{2,1,0:T(8,128)(2,1)S(1)}, u32[]{:S(2)}, u32[]{:S(2)}) async-start(bf16[8,32,256]{2,1,0:T(8,128)(2,1)} %broadcast_select_fusion.1), calls=%async_computation | async-start | bytes 262144 | tf_op jit(solution)/shard_map/all_to_all | solution.py:75
  29.3 4.0 %copy-start.13 = (s32[1,1,16,2]{2,3,1,0:T(2,128)S(1)}, s32[1,1,16,2]{2,3,1,0:T(2,128)}, u32[]{:S(2)}) copy-start(s32[1,1,16,2]{2,3,1,0:T(2,128)} %param.24) | copy-start | bytes 388
  29.3 4.0 %copy-start.12 = (s32[1,1,16,3]{2,1,3,0:T(1,128)S(1)}, s32[1,1,16,3]{2,1,3,0:T(1,128)}, u32[]{:S(2)}) copy-start(s32[1,1,16,3]{2,1,3,0:T(1,128)} %param.22) | copy-start | bytes 580
  29.3 4.1 %copy-start.14 = (s32[1,1,16,2]{2,3,1,0:T(2,128)S(1)}, s32[1,1,16,2]{2,3,1,0:T(2,128)}, u32[]{:S(2)}) copy-start(s32[1,1,16,2]{2,3,1,0:T(2,128)} %param.26) | copy-start | bytes 388
  34.0 5.9 %collective-permute-start.1 = (bf16[256,256]{1,0:T(8,128)(2,1)S(1)}, bf16[256,256]{1,0:T(8,128)(2,1)S(1)}, u32[]{:S(2)}, u32[]{:S(2)}) collective-permute-start(bf16[256,256]{1,0:T(8,128)(2,1)S(1)} %collective-permute-done), channel_id=1, source_target_pairs={{0,1},{1,2},{2,3},{3,0},{4,5},{5,6},{6,7},{7,4},{8,9},{9,10},{10,1... | collective-permute-start | bytes 393224 | tf_op jit(solution)/shard_map/ppermute | solution.py:14
  36.2 3.9 %copy-start.8 = (bf16[256,256]{1,0:T(8,128)(2,1)S(1)}, bf16[256,256]{1,0:T(8,128)(2,1)}, u32[]{:S(2)}) copy-start(bf16[256,256]{1,0:T(8,128)(2,1)} %param.16) | copy-start | bytes 393220
  42.2 4.2 %copy-start.15 = (bf16[1,1,2048,256]{3,2,1,0:T(8,128)(2,1)S(1)}, bf16[1,1,2048,256]{3,2,1,0:T(8,128)(2,1)}, u32[]{:S(2)}) copy-start(bf16[1,1,2048,256]{3,2,1,0:T(8,128)(2,1)} %param.29) | copy-start | bytes 3145732
  46.1 1.6 copy-start.7
  46.1 1.6 copy-start.11
  46.1 1.6 copy-start.16
  49.9 2.4 copy-start.3
  51.2 1.7 copy-start.5
  52.8 2.8 copy-start.6
  118.6 27.4 %all-to-all-start.1 = ((f32[8,32,256]{2,1,0:T(8,128)}), f32[8,32,256]{2,1,0:T(8,128)S(1)}, u32[]{:S(2)}, u32[]{:S(2)}) async-start(f32[8,32,256]{2,1,0:T(8,128)} %reshape.247), calls=%async_computation.1 | async-start | bytes 524288 | tf_op jit(solution)/shard_map/all_to_all | solution.py:126
  123.8 150.7 %all-reduce.3.cloned.1.call-start = ((), (), s32[]{:S(2)}) async-start(), calls=%async_computation.2 | async-start | bytes 3145728 | tf_op jit(solution)/shard_map/psum | solution.py:110
  136.2 4.6 %copy-start.9 = (bf16[256,256]{1,0:T(8,128)(2,1)S(1)}, bf16[256,256]{1,0:T(8,128)(2,1)}, u32[]{:S(2)}) copy-start(bf16[256,256]{1,0:T(8,128)(2,1)} %param.17) | copy-start | bytes 393220
  140.8 1.2 copy-start.4
  150.9 128.6 %copy-start.1 = (bf16[1,1,16,3,128,128]{5,4,3,2,1,0:T(8,128)(2,1)S(1)}, bf16[1,1,16,3,128,128]{5,4,3,2,1,0:T(8,128)(2,1)}, u32[]{:S(2)}) copy-start(bf16[1,1,16,3,128,128]{5,4,3,2,1,0:T(8,128)(2,1)} %param.23) | copy-start | bytes 4718596
  274.6 4.1 %copy-start.10 = (f32[256,256]{0,1:T(8,128)S(1)}, f32[256,256]{0,1:T(8,128)}, u32[]{:S(2)}) copy-start(f32[256,256]{0,1:T(8,128)} %get-tuple-element.19) | copy-start | bytes 786436
Sparse Core Ops, SparseCore 0:
  141.0 133.5 all-reduce.2
